TPU v7x, 32 devices: a whole 2x2x4 slice. The times are simulated.
32 devices in a mesh: cand: 4 (over x, core), seq: 8 (over z, y).
Axes of the slice: x: 2, y: 2, z: 4, core: 2. Of those that a mesh axis runs over, the one named last changes fastest.
Arguments:
- response_query_array: bfloat16 [8, 768, 2560], P('cand', 'seq'), may hold values from -180 to 180
- response_key_array: bfloat16 [8, 768, 512], P('cand', 'seq'), may hold values from -6 to 6
- response_value_array: bfloat16 [8, 768, 512], P('cand', 'seq'), may hold values from -6 to 6
- prompt_key_array: bfloat16 [2048, 512], P(('cand', 'seq')), may hold values from -6 to 6
- prompt_value_array: bfloat16 [2048, 512], P(('cand', 'seq')), may hold values from -6 to 6
- lengths: int32 [8], replicated, may hold values from 192 to 768, as said below
- offsets: int32 [8], replicated, may hold values from 512 to 2048, as said below
- ranks: int32 [8], replicated, may hold values from 0 to 7, each once
Outputs:
- attention: bfloat16 [8, 768, 2560], P('cand', 'seq')
Inputs may be any that keep to these rules, and one draw needn't show every extreme that they name: `lengths`: some candidate's response has all 768 positions live. `offsets`: some candidate sees the whole prompt.
All inputs are finite; a program needn't handle non-finite values.
Results may differ from a plain program's by a relative error of at most 0.004.
Values may be sent and summed in bfloat16 or wider, within the bound.
No kernel may reach another device: no remote copies, remote signals or barrier semaphores. Data moves between devices by JAX's collectives and lax.ppermute only.
A program may use at most 128 MiB of HBM per device.

v0:
```python
import math
import jax
import jax.numpy as jnp
from jax import lax
from jax.sharding import PartitionSpec as P

QUERY_HEADS = 20
KEY_VALUE_HEADS = 4
HEAD_DIMENSION = 128
lowest_score_value = -1e30


def attend_block(running, query_rows, block_keys, block_values, allowed, shared):
    running_max, running_total, running_sum = running
    cand_count = query_rows.shape[0]
    heads_kv = query_rows.shape[2]
    head_size = query_rows.shape[4]
    score_scale = 1.0 / math.sqrt(head_size)
    if shared:
        keys_split = block_keys.reshape(block_keys.shape[0], heads_kv, head_size)
        values_split = block_values.reshape(block_values.shape[0], heads_kv, head_size)
        scores = jnp.einsum(
            "crhgd,nhd->chgrn", query_rows, keys_split, preferred_element_type=jnp.float32
        )
    else:
        keys_split = block_keys.reshape(cand_count, block_keys.shape[1], heads_kv, head_size)
        values_split = block_values.reshape(cand_count, block_values.shape[1], heads_kv, head_size)
        scores = jnp.einsum(
            "crhgd,cnhd->chgrn", query_rows, keys_split, preferred_element_type=jnp.float32
        )
    scores = jnp.where(allowed[:, None, None, :, :], scores * score_scale, -jnp.inf)
    new_max = jnp.maximum(running_max, jnp.max(scores, axis=-1))
    rescale = jnp.exp(running_max - new_max)
    exponent = jnp.exp(scores - new_max[..., None])
    weights = exponent.astype(jnp.bfloat16)
    new_total = running_total * rescale + jnp.sum(exponent, axis=-1)
    if shared:
        contrib = jnp.einsum(
            "chgrn,nhd->chgrd", weights, values_split, preferred_element_type=jnp.float32
        )
    else:
        contrib = jnp.einsum(
            "chgrn,cnhd->chgrd", weights, values_split, preferred_element_type=jnp.float32
        )
    new_sum = running_sum * rescale[..., None] + contrib
    return (new_max, new_total, new_sum)


def fold_blocks(
    running, query_rows, all_keys, all_values, key_pos, allowed_of, shared, live_of=None
):
    key_count = key_pos.shape[0]
    block_len = math.gcd(key_count, 512)
    keys_axis = 0 if shared else 1

    def one_block(step_at, carried):
        block_start = step_at * block_len
        block_keys = lax.dynamic_slice_in_dim(all_keys, block_start, block_len, keys_axis)
        block_values = lax.dynamic_slice_in_dim(all_values, block_start, block_len, keys_axis)
        block_pos = lax.dynamic_slice_in_dim(key_pos, block_start, block_len, 0)
        return attend_block(
            carried, query_rows, block_keys, block_values, allowed_of(block_pos), shared
        )

    return lax.fori_loop(0, key_count // block_len, one_block, running)


def body(
    response_query_array,
    response_key_array,
    response_value_array,
    prompt_key_array,
    prompt_value_array,
    lengths,
    offsets,
    ranks,
):
    candidate_local, output_rows, width = response_query_array.shape
    group_width = QUERY_HEADS // KEY_VALUE_HEADS
    group_at = lax.axis_index("cand")
    seq_at = lax.axis_index("seq")
    first_cand = group_at * candidate_local
    my_lengths = lax.dynamic_slice_in_dim(lengths, first_cand, candidate_local)
    my_offsets = lax.dynamic_slice_in_dim(offsets, first_cand, candidate_local)
    query_pos = seq_at * output_rows + jnp.arange(output_rows, dtype=jnp.int32)
    query_rows = response_query_array.reshape(
        candidate_local, output_rows, KEY_VALUE_HEADS, group_width, HEAD_DIMENSION
    )
    pieces = (
        lax.all_gather(prompt_key_array, ("cand", "seq"), axis=0, tiled=True),
        lax.all_gather(prompt_value_array, ("cand", "seq"), axis=0, tiled=True),
    )
    key_pos = jnp.arange(pieces[0].shape[0], dtype=jnp.int32)

    def allowed_of(block_pos):
        return block_pos[None, None, :] < my_offsets[:, None, None]

    running = fold_blocks(
        (
            jnp.full(
                (candidate_local, KEY_VALUE_HEADS, group_width, output_rows),
                lowest_score_value,
                jnp.float32,
            ),
            jnp.zeros((candidate_local, KEY_VALUE_HEADS, group_width, output_rows), jnp.float32),
            jnp.zeros(
                (candidate_local, KEY_VALUE_HEADS, group_width, output_rows, HEAD_DIMENSION),
                jnp.float32,
            ),
        ),
        query_rows,
        pieces[0],
        pieces[1],
        key_pos,
        allowed_of,
        True,
    )
    pieces = (
        lax.all_gather(response_key_array, "seq", axis=1, tiled=True),
        lax.all_gather(response_value_array, "seq", axis=1, tiled=True),
    )
    key_pos = jnp.arange(pieces[0].shape[1], dtype=jnp.int32)

    def allowed_of(block_pos):
        causal = block_pos[None, None, :] <= query_pos[None, :, None]
        return causal & (block_pos[None, None, :] < my_lengths[:, None, None])

    final_max, final_total, final_sum = fold_blocks(
        running, query_rows, pieces[0], pieces[1], key_pos, allowed_of, False
    )
    attended = final_sum / final_total[..., None]
    attended = jnp.transpose(attended, (0, 3, 1, 2, 4)).reshape(candidate_local, output_rows, width)
    row_valid = query_pos[None, :] < my_lengths[:, None]
    attended = jnp.where(row_valid[:, :, None], attended, 0.0).astype(jnp.bfloat16)
    gathered = lax.all_gather(attended, "cand", axis=0, tiled=True)
    every_cand = jnp.arange(gathered.shape[0], dtype=jnp.int32)
    chosen = []
    for within in range(candidate_local):
        target = first_cand + within
        source = jnp.sum(jnp.where(ranks == target, every_cand, 0))
        chosen.append(lax.dynamic_index_in_dim(gathered, source, 0, keepdims=False))
    return jnp.stack(chosen, axis=0)


def solution(mesh):
    in_specs = (
        P("cand", "seq", None),
        P("cand", "seq", None),
        P("cand", "seq", None),
        P(("cand", "seq"), None),
        P(("cand", "seq"), None),
        P(),
        P(),
        P(),
    )
    out_specs = P("cand", "seq", None)
    return jax.shard_map(body, mesh=mesh, in_specs=in_specs, out_specs=out_specs, check_vma=False)
```

profile of v0, /device:TPU:0, one launch (start us, length us, event | category | flops | bytes accessed | tf_op | source)
XLA Modules:
  0.0 304.9 jit_solution(10088347945177968936)
XLA Ops:
  6.5 0.7 all-gather.6.cloned.1.call-update
  7.3 0.7 all-gather.8.cloned.1.call-update
  8.1 1.8 copy.56
  9.9 1.8 copy.57
  11.9 1.7 copy.52
  13.6 0.7 copy.54
  14.3 1.4 copy.62
  15.9 53.7 %all-gather.6.cloned.1.call-done = bf16[2048,512]{1,0:T(8,128)(2,1)} async-done(((bf16[64,512]{1,0:T(8,128)(2,1)}), bf16[2048,512]{1,0:T(8,128)(2,1)}) %all-gather.6.cloned.1.call-update) | async-done | bytes 2097168 | tf_op jit(solution)/shard_map/all_gather | solution.py:90
  69.6 58.4 %all-gather.8.cloned.1.call-done = bf16[2048,512]{1,0:T(8,128)(2,1)} async-done(((bf16[64,512]{1,0:T(8,128)(2,1)}), bf16[2048,512]{1,0:T(8,128)(2,1)}) %all-gather.8.cloned.1.call-update) | async-done | bytes 2097168 | tf_op jit(solution)/shard_map/all_gather | solution.py:91
  128.0 65.4 %while.37 = (s32[]{:T(128)}, f32[2,4,5,96]{3,2,0,1:T(8,128)S(1)}, f32[2,4,5,96]{3,2,0,1:T(8,128)S(1)}, f32[2,4,5,96,128]{4,3,2,0,1:T(8,128)}, s32[2048]{0:T(1024...) while((s32[]{:T(128)}, f32[2,4,5,96]{3,2,0,1:T(8,128)S(1)}, ...), condition=%wide.region_3.4_spmd.clone, body=%wide.region_0.3_spmd.clone.sunk | while | flops 1029754624 | bytes 34007236 | solution.py:65
  128.1 1.3 constant_dynamic-slice_fusion.9
  129.6 4.2 %fusion.60 = (f32[2,4,5,96]{3,2,0,1:T(8,128)S(1)}, f32[4,512,2,96,5]{1,3,4,2,0:T(8,128)}) fusion(pred[2,512]{1,0:T(4,128)(4,1)S(1)} %broadcast_compare_fusion.9, bf16[512,4,128,1,1]{0,2,4,3,1:T(8,128)(2,1)S(1)} %bitcast.88, bf16[2,96,4,5,128]{4,1,3,0,2:T(8,128)(2,1)S(1)} %get-tuple-element.683), kind=kOutput, calls=%fused_computation.26.clone.1 | convolution fusion | flops 509210880 | bytes 9388032 | tf_op jit(solution)/shard_map/while/body/eval_jaxpr/crhgd,nhd->chgrn/dot_general | solution.py:22
  133.9 4.5 %fusion.61 = f32[2,4,5,96]{3,2,0,1:T(8,128)S(1)} fusion(f32[4,512,2,96,5]{1,3,4,2,0:T(8,128)} %get-tuple-element.646, f32[2,4,5,96]{3,2,0,1:T(8,128)S(1)} %select_maximum_fusion.2, pred[2,512]{1,0:T(4,128)(4,1)S(1)} %broadcast_compare_fusion.9), kind=kLoop, calls=%fused_computation.25.clone.1 | loop fusion | flops 7860480 | bytes 7896064 | tf_op jit(solution)/shard_map/while/body/eval_jaxpr/reduce_sum | solution.py:36
  138.6 5.4 %bitcast_add_fusion.2 = f32[2,4,5,96,128]{4,3,2,0,1:T(8,128)} fusion(f32[2,4,5,96,128]{4,3,2,0,1:T(8,128)} %get-tuple-element.666, bf16[512,4,128,1,1]{0,2,4,3,1:T(8,128)(2,1)S(1)} %bitcast.91, f32[4,512,2,96,5]{1,3,4,2,0:T(8,128)} %get-tuple-element.646, f32[2,4,5,96]{3,2,0,1:T(8,128)S(1)} %select_maximum_fusion.2, ...), kind=kOutput, calls=%fused_computation.32.clone.1 | convolution fusion | flops 512655360 | bytes 12352513 | tf_op jit(solution)/shard_map/while/body/eval_jaxpr/chgrn,nhd->chgrd/dot_general | solution.py:38
  144.2 1.3 constant_dynamic-slice_fusion.9
  145.7 4.2 %fusion.60 = (f32[2,4,5,96]{3,2,0,1:T(8,128)S(1)}, f32[4,512,2,96,5]{1,3,4,2,0:T(8,128)}) fusion(pred[2,512]{1,0:T(4,128)(4,1)S(1)} %broadcast_compare_fusion.9, bf16[512,4,128,1,1]{0,2,4,3,1:T(8,128)(2,1)S(1)} %bitcast.88, bf16[2,96,4,5,128]{4,1,3,0,2:T(8,128)(2,1)S(1)} %get-tuple-element.683), kind=kOutput, calls=%fused_computation.26.clone.1 | convolution fusion | flops 509210880 | bytes 9388032 | tf_op jit(solution)/shard_map/while/body/eval_jaxpr/crhgd,nhd->chgrn/dot_general | solution.py:22
  149.9 4.4 %fusion.61 = f32[2,4,5,96]{3,2,0,1:T(8,128)S(1)} fusion(f32[4,512,2,96,5]{1,3,4,2,0:T(8,128)} %get-tuple-element.646, f32[2,4,5,96]{3,2,0,1:T(8,128)S(1)} %select_maximum_fusion.2, pred[2,512]{1,0:T(4,128)(4,1)S(1)} %broadcast_compare_fusion.9), kind=kLoop, calls=%fused_computation.25.clone.1 | loop fusion | flops 7860480 | bytes 7896064 | tf_op jit(solution)/shard_map/while/body/eval_jaxpr/reduce_sum | solution.py:36
  154.6 6.0 %bitcast_add_fusion.2 = f32[2,4,5,96,128]{4,3,2,0,1:T(8,128)} fusion(f32[2,4,5,96,128]{4,3,2,0,1:T(8,128)} %get-tuple-element.666, bf16[512,4,128,1,1]{0,2,4,3,1:T(8,128)(2,1)S(1)} %bitcast.91, f32[4,512,2,96,5]{1,3,4,2,0:T(8,128)} %get-tuple-element.646, f32[2,4,5,96]{3,2,0,1:T(8,128)S(1)} %select_maximum_fusion.2, ...), kind=kOutput, calls=%fused_computation.32.clone.1 | convolution fusion | flops 512655360 | bytes 12352513 | tf_op jit(solution)/shard_map/while/body/eval_jaxpr/chgrn,nhd->chgrd/dot_general | solution.py:38
  160.7 1.3 constant_dynamic-slice_fusion.9
  162.2 4.2 %fusion.60 = (f32[2,4,5,96]{3,2,0,1:T(8,128)S(1)}, f32[4,512,2,96,5]{1,3,4,2,0:T(8,128)}) fusion(pred[2,512]{1,0:T(4,128)(4,1)S(1)} %broadcast_compare_fusion.9, bf16[512,4,128,1,1]{0,2,4,3,1:T(8,128)(2,1)S(1)} %bitcast.88, bf16[2,96,4,5,128]{4,1,3,0,2:T(8,128)(2,1)S(1)} %get-tuple-element.683), kind=kOutput, calls=%fused_computation.26.clone.1 | convolution fusion | flops 509210880 | bytes 9388032 | tf_op jit(solution)/shard_map/while/body/eval_jaxpr/crhgd,nhd->chgrn/dot_general | solution.py:22
  166.4 4.4 %fusion.61 = f32[2,4,5,96]{3,2,0,1:T(8,128)S(1)} fusion(f32[4,512,2,96,5]{1,3,4,2,0:T(8,128)} %get-tuple-element.646, f32[2,4,5,96]{3,2,0,1:T(8,128)S(1)} %select_maximum_fusion.2, pred[2,512]{1,0:T(4,128)(4,1)S(1)} %broadcast_compare_fusion.9), kind=kLoop, calls=%fused_computation.25.clone.1 | loop fusion | flops 7860480 | bytes 7896064 | tf_op jit(solution)/shard_map/while/body/eval_jaxpr/reduce_sum | solution.py:36
  171.1 5.9 %bitcast_add_fusion.2 = f32[2,4,5,96,128]{4,3,2,0,1:T(8,128)} fusion(f32[2,4,5,96,128]{4,3,2,0,1:T(8,128)} %get-tuple-element.666, bf16[512,4,128,1,1]{0,2,4,3,1:T(8,128)(2,1)S(1)} %bitcast.91, f32[4,512,2,96,5]{1,3,4,2,0:T(8,128)} %get-tuple-element.646, f32[2,4,5,96]{3,2,0,1:T(8,128)S(1)} %select_maximum_fusion.2, ...), kind=kOutput, calls=%fused_computation.32.clone.1 | convolution fusion | flops 512655360 | bytes 12352513 | tf_op jit(solution)/shard_map/while/body/eval_jaxpr/chgrn,nhd->chgrd/dot_general | solution.py:38
  177.1 1.3 constant_dynamic-slice_fusion.9
  178.6 4.2 %fusion.60 = (f32[2,4,5,96]{3,2,0,1:T(8,128)S(1)}, f32[4,512,2,96,5]{1,3,4,2,0:T(8,128)}) fusion(pred[2,512]{1,0:T(4,128)(4,1)S(1)} %broadcast_compare_fusion.9, bf16[512,4,128,1,1]{0,2,4,3,1:T(8,128)(2,1)S(1)} %bitcast.88, bf16[2,96,4,5,128]{4,1,3,0,2:T(8,128)(2,1)S(1)} %get-tuple-element.683), kind=kOutput, calls=%fused_computation.26.clone.1 | convolution fusion | flops 509210880 | bytes 9388032 | tf_op jit(solution)/shard_map/while/body/eval_jaxpr/crhgd,nhd->chgrn/dot_general | solution.py:22
  182.8 4.4 %fusion.61 = f32[2,4,5,96]{3,2,0,1:T(8,128)S(1)} fusion(f32[4,512,2,96,5]{1,3,4,2,0:T(8,128)} %get-tuple-element.646, f32[2,4,5,96]{3,2,0,1:T(8,128)S(1)} %select_maximum_fusion.2, pred[2,512]{1,0:T(4,128)(4,1)S(1)} %broadcast_compare_fusion.9), kind=kLoop, calls=%fused_computation.25.clone.1 | loop fusion | flops 7860480 | bytes 7896064 | tf_op jit(solution)/shard_map/while/body/eval_jaxpr/reduce_sum | solution.py:36
  187.5 5.9 %bitcast_add_fusion.2 = f32[2,4,5,96,128]{4,3,2,0,1:T(8,128)} fusion(f32[2,4,5,96,128]{4,3,2,0,1:T(8,128)} %get-tuple-element.666, bf16[512,4,128,1,1]{0,2,4,3,1:T(8,128)(2,1)S(1)} %bitcast.91, f32[4,512,2,96,5]{1,3,4,2,0:T(8,128)} %get-tuple-element.646, f32[2,4,5,96]{3,2,0,1:T(8,128)S(1)} %select_maximum_fusion.2, ...), kind=kOutput, calls=%fused_computation.32.clone.1 | convolution fusion | flops 512655360 | bytes 12352513 | tf_op jit(solution)/shard_map/while/body/eval_jaxpr/chgrn,nhd->chgrd/dot_general | solution.py:38
  193.4 1.7 copy.60
  195.1 0.6 copy.58
  195.7 0.6 copy.59
  196.3 22.1 %all-gather.12.cloned.1.call-done = bf16[2,768,512]{2,0,1:T(2,128)(2,1)} async-done(((bf16[2,96,512]{2,0,1:T(2,128)(2,1)}), bf16[2,768,512]{2,0,1:T(2,128)(2,1)}) %all-gather.12.cloned.1.call-update) | async-done | bytes 1572880 | tf_op jit(solution)/shard_map/all_gather | solution.py:120
  218.4 41.8 %while.36 = (s32[]{:T(128)}, f32[2,4,5,96]{3,2,1,0:T(8,128)}, f32[2,4,5,96]{3,2,1,0:T(8,128)}, f32[2,4,5,96,128]{4,3,2,1,0:T(8,128)S(1)}, s32[768]{0:T(1024)S(1)...) while((s32[]{:T(128)}, f32[2,4,5,96]{3,2,1,0:T(8,128)}, ...), condition=%wide.region_7.8_spmd.clone, body=%wide.region_4.7_spmd.clone.sunk | while | flops 515194976 | bytes 38561872 | solution.py:65
  218.6 0.7 broadcast_and_fusion.2
  219.3 1.9 constant_dynamic-slice_fusion.8
  221.2 0.5 copy.86
  221.8 2.2 fusion.54
  224.0 1.8 copy-done
  225.9 1.5 fusion.55
  227.5 0.5 copy.87
  228.0 3.7 %multiply_add_fusion.5 = f32[2,4,5,96,128]{4,3,2,1,0:T(8,128)S(1)} fusion(f32[2,4,5,96,128]{4,3,2,1,0:T(8,128)S(1)} %get-tuple-element.706, bf16[2,256,4,128,1]{1,3,4,2,0:T(8,128)(2,1)S(1)} %bitcast.89, f32[2,4,256,96,5]{2,3,4,1,0:T(8,128)} %copy-done, f32[2,4,5,96]{3,2,1,0:T(8,128)S(1)} %max.19, pred[2,96,256]{2,1,0:T(8,128)(4,1)S(1)} %copy-done.1, ...), kind=kOutput, calls=%fused_computation.7.clone.1 | convolution fusion | flops 256573440 | bytes 8468480 | tf_op jit(solution)/shard_map/while/body/eval_jaxpr/chgrn,cnhd->chgrd/dot_general | solution.py:42
  231.7 0.6 copy.111
  232.6 0.7 broadcast_and_fusion.2
  233.2 1.9 constant_dynamic-slice_fusion.8
  235.2 0.5 copy.86
  235.7 2.2 fusion.54
  238.0 1.8 copy-done
  239.8 1.5 fusion.55
  241.9 3.7 %multiply_add_fusion.5 = f32[2,4,5,96,128]{4,3,2,1,0:T(8,128)S(1)} fusion(f32[2,4,5,96,128]{4,3,2,1,0:T(8,128)S(1)} %get-tuple-element.706, bf16[2,256,4,128,1]{1,3,4,2,0:T(8,128)(2,1)S(1)} %bitcast.89, f32[2,4,256,96,5]{2,3,4,1,0:T(8,128)} %copy-done, f32[2,4,5,96]{3,2,1,0:T(8,128)S(1)} %max.19, pred[2,96,256]{2,1,0:T(8,128)(4,1)S(1)} %copy-done.1, ...), kind=kOutput, calls=%fused_computation.7.clone.1 | convolution fusion | flops 256573440 | bytes 8468480 | tf_op jit(solution)/shard_map/while/body/eval_jaxpr/chgrn,cnhd->chgrd/dot_general | solution.py:42
  245.6 0.6 copy.111
  246.5 0.7 broadcast_and_fusion.2
  247.2 1.9 constant_dynamic-slice_fusion.8
  249.1 0.5 copy.86
  249.7 2.2 fusion.54
  251.9 1.8 copy-done
  253.7 1.5 fusion.55
  255.9 3.7 %multiply_add_fusion.5 = f32[2,4,5,96,128]{4,3,2,1,0:T(8,128)S(1)} fusion(f32[2,4,5,96,128]{4,3,2,1,0:T(8,128)S(1)} %get-tuple-element.706, bf16[2,256,4,128,1]{1,3,4,2,0:T(8,128)(2,1)S(1)} %bitcast.89, f32[2,4,256,96,5]{2,3,4,1,0:T(8,128)} %copy-done, f32[2,4,5,96]{3,2,1,0:T(8,128)S(1)} %max.19, pred[2,96,256]{2,1,0:T(8,128)(4,1)S(1)} %copy-done.1, ...), kind=kOutput, calls=%fused_computation.7.clone.1 | convolution fusion | flops 256573440 | bytes 8468480 | tf_op jit(solution)/shard_map/while/body/eval_jaxpr/chgrn,cnhd->chgrd/dot_general | solution.py:42
  259.6 0.6 copy.111
  260.2 1.3 divide_bitcast_fusion
  261.5 0.8 copy.64
  262.3 0.6 copy.65
  262.9 1.2 select_convert_fusion
  264.2 0.7 fusion.29
  268.5 27.6 %all-gather.14.cloned.1.call-done = bf16[8,96,2560]{2,1,0:T(8,128)(2,1)} async-done(((bf16[2,96,2560]{2,1,0:T(8,128)(2,1)}), bf16[8,96,2560]{2,1,0:T(8,128)(2,1)}) %all-gather.14.cloned.1.call-update) | async-done | bytes 3932176 | tf_op jit(solution)/shard_map/all_gather | solution.py:135
  296.1 1.2 constant_dynamic-slice_fusion.5
  297.3 1.0 pad_maximum_fusion
  (99 shorter events, 4.9 us)
Async XLA Ops:
  6.5 63.1 %all-gather.6.cloned.1.call-start = ((), (), s32[]{:S(2)}) async-start(), calls=%async_computation | async-start | bytes 2162688 | tf_op jit(solution)/shard_map/all_gather | solution.py:90
  7.3 120.7 %all-gather.8.cloned.1.call-start = ((), (), s32[]{:S(2)}) async-start(), calls=%async_computation.1 | async-start | bytes 2162688 | tf_op jit(solution)/shard_map/all_gather | solution.py:91
  8.0 188.3 %all-gather.10.cloned.1.call-start = ((), (), s32[]{:S(2)}) async-start(), calls=%async_computation.2 | async-start | bytes 1769472 | tf_op jit(solution)/shard_map/all_gather | solution.py:119
  9.9 5.8 %copy-start.6 = (s32[8]{0:T(128)S(1)}, s32[8]{0:T(128)}, u32[]{:S(2)}) copy-start(s32[8]{0:T(128)} %param.18) | copy-start | bytes 100
  9.9 5.9 %copy-start.7 = (s32[8]{0:T(128)S(1)}, s32[8]{0:T(128)}, u32[]{:S(2)}) copy-start(s32[8]{0:T(128)} %param.17) | copy-start | bytes 100
  9.9 208.5 %all-gather.12.cloned.1.call-start = ((), (), s32[]{:S(2)}) async-start(), calls=%async_computation.3 | async-start | bytes 1769472 | tf_op jit(solution)/shard_map/all_gather | solution.py:120
  11.8 284.3 %all-gather.14.cloned.1.call-start = ((), (), s32[]{:S(2)}) async-start(), calls=%async_computation.4 | async-start | bytes 4915200 | tf_op jit(solution)/shard_map/all_gather | solution.py:135
  221.8 2.2 copy-start.2
  221.8 4.1 %copy-start.1 = (pred[2,96,256]{2,1,0:T(8,128)(4,1)S(1)}, pred[2,96,256]{2,1,0:T(8,128)(4,1)}, u32[]{:S(2)}) copy-start(pred[2,96,256]{2,1,0:T(8,128)(4,1)} %broadcast_and_fusion.2) | copy-start | bytes 147460 | tf_op jit(solution)/shard_map/while
  221.8 5.6 %copy-start.3 = (f32[2,4,5,96]{3,2,1,0:T(8,128)S(1)}, f32[2,4,5,96]{3,2,1,0:T(8,128)}, u32[]{:S(2)}) copy-start(f32[2,4,5,96]{3,2,1,0:T(8,128)} %get-tuple-element.705) | copy-start | bytes 46084 | tf_op jit(solution)/shard_map/while
  224.0 1.8 copy-start
  227.4 4.3 %copy-start.4 = (f32[2,4,5,96]{3,2,1,0:T(8,128)}, f32[2,4,5,96]{3,2,1,0:T(8,128)S(1)}, u32[]{:S(2)}) copy-start(f32[2,4,5,96]{3,2,1,0:T(8,128)S(1)} %get-tuple-element.719) | copy-start | bytes 46084 | tf_op jit(solution)/shard_map/while
  235.7 2.2 copy-start.2
  235.7 4.1 %copy-start.1 = (pred[2,96,256]{2,1,0:T(8,128)(4,1)S(1)}, pred[2,96,256]{2,1,0:T(8,128)(4,1)}, u32[]{:S(2)}) copy-start(pred[2,96,256]{2,1,0:T(8,128)(4,1)} %broadcast_and_fusion.2) | copy-start | bytes 147460 | tf_op jit(solution)/shard_map/while
  235.7 5.6 %copy-start.3 = (f32[2,4,5,96]{3,2,1,0:T(8,128)S(1)}, f32[2,4,5,96]{3,2,1,0:T(8,128)}, u32[]{:S(2)}) copy-start(f32[2,4,5,96]{3,2,1,0:T(8,128)} %get-tuple-element.705) | copy-start | bytes 46084 | tf_op jit(solution)/shard_map/while
  237.9 1.8 copy-start
  241.4 4.3 %copy-start.4 = (f32[2,4,5,96]{3,2,1,0:T(8,128)}, f32[2,4,5,96]{3,2,1,0:T(8,128)S(1)}, u32[]{:S(2)}) copy-start(f32[2,4,5,96]{3,2,1,0:T(8,128)S(1)} %get-tuple-element.719) | copy-start | bytes 46084 | tf_op jit(solution)/shard_map/while
  249.6 2.2 copy-start.2
  249.6 4.1 %copy-start.1 = (pred[2,96,256]{2,1,0:T(8,128)(4,1)S(1)}, pred[2,96,256]{2,1,0:T(8,128)(4,1)}, u32[]{:S(2)}) copy-start(pred[2,96,256]{2,1,0:T(8,128)(4,1)} %broadcast_and_fusion.2) | copy-start | bytes 147460 | tf_op jit(solution)/shard_map/while
  249.7 5.6 %copy-start.3 = (f32[2,4,5,96]{3,2,1,0:T(8,128)S(1)}, f32[2,4,5,96]{3,2,1,0:T(8,128)}, u32[]{:S(2)}) copy-start(f32[2,4,5,96]{3,2,1,0:T(8,128)} %get-tuple-element.705) | copy-start | bytes 46084 | tf_op jit(solution)/shard_map/while
  251.9 1.8 copy-start
  255.3 4.3 %copy-start.4 = (f32[2,4,5,96]{3,2,1,0:T(8,128)}, f32[2,4,5,96]{3,2,1,0:T(8,128)S(1)}, u32[]{:S(2)}) copy-start(f32[2,4,5,96]{3,2,1,0:T(8,128)S(1)} %get-tuple-element.719) | copy-start | bytes 46084 | tf_op jit(solution)/shard_map/while
  261.5 2.6 copy-start.5
Sparse Core Ops, SparseCore 0:
  10.3 59.2 all-gather.5
  72.6 55.3 all-gather.7
  130.2 43.0 all-gather.9
  175.3 43.0 all-gather.11
  264.3 31.7 all-gather.13
where the time goes:
time: 306 us; the launch traced here: 305 us
  waiting for transfers between devices  163 us (53%)
  matrix products  57.7 us (19%)
  local copies, waits for them, and re-layouts  36.7 us (12%)
  other arithmetic  29.6 us (10%)
  between operations  16.9 us (6%)
    all_gather x1, waiting for transfers between devices, body(): lax.all_gather(prompt_value_array, ('cand', 'seq'), axis=0, tiled=True)  58.4 us
    all_gather x1, waiting for transfers between devices, body(): lax.all_gather(prompt_key_array, ('cand', 'seq'), axis=0, tiled=True)  53.7 us
    all_gather x1, waiting for transfers between devices, body(): gathered = lax.all_gather(attended, 'cand', axis=0, tiled=True)  27.6 us
    dot_general x4, matrix products, attend_block(): jnp.einsum('chgrn,nhd->chgrd', weights, values_split, preferred_element_t...  23.1 us
    reduce_sum x7, other arithmetic, attend_block(): new_total = running_total * rescale + jnp.sum(exponent, axis=-1)  22.3 us
    all_gather x1, waiting for transfers between devices, body(): lax.all_gather(response_value_array, 'seq', axis=1, tiled=True)  22.1 us
    dot_general x4, matrix products, attend_block(): jnp.einsum('crhgd,nhd->chgrn', query_rows, keys_split, preferred_element_...  16.9 us
    dynamic_slice x14, local copies, waits for them, and re-layouts, one_block(): lax.dynamic_slice_in_dim(all_values, block_start, block_len, keys_axis)  13.3 us
  transfers between devices with their start and end apart: 5, of which 4 were waited for; matrix products, arithmetic and copies ran while one was open for 25% of the time, Pallas kernels for 0%

commit v1 on v0

--- a/solution.py
+++ b/solution.py
@@ -1,3 +1,4 @@
+import functools
 import math
 import jax
 import jax.numpy as jnp
@@ -8,6 +9,21 @@
 KEY_VALUE_HEADS = 4
 HEAD_DIMENSION = 128
 lowest_score_value = -1e30
+
+
+def patch_proceed(unit, mesh_name):
+    total_devices = lax.axis_size(mesh_name)
+    aux = [(rr - 1, rr) for rr in range(1, total_devices)] + [(total_devices - 1, 0)]
+    h_now = unit
+    trail = [h_now]
+    for _ in range(total_devices - 1):
+        h_now = lax.ppermute(h_now, mesh_name, aux)
+        trail += [h_now]
+    known = jnp.concatenate([*reversed(trail)], axis=0)
+    return jnp.roll(known, (lax.axis_index(mesh_name) + 1) * h_now.shape[0], axis=0)
+
+
+connect_targets_on_mesh = functools.partial(patch_proceed, mesh_name="cand")
 
 
 def attend_block(running, query_rows, block_keys, block_values, allowed, shared):
@@ -132,7 +148,7 @@
     attended = jnp.transpose(attended, (0, 3, 1, 2, 4)).reshape(candidate_local, output_rows, width)
     row_valid = query_pos[None, :] < my_lengths[:, None]
     attended = jnp.where(row_valid[:, :, None], attended, 0.0).astype(jnp.bfloat16)
-    gathered = lax.all_gather(attended, "cand", axis=0, tiled=True)
+    gathered = connect_targets_on_mesh(attended)
     every_cand = jnp.arange(gathered.shape[0], dtype=jnp.int32)
     chosen = []
     for within in range(candidate_local):

time: 306 us -> 313 us (1.023)
  waiting for transfers between devices: 163 us -> 197 us
  matrix products: 57.7 us -> 27 us
  local copies, waits for them, and re-layouts: 36.7 us -> 49.8 us
  other arithmetic: 29.6 us -> 20.2 us
    ppermute x0 -> x3, waiting for transfers between devices: none -> 32.4 us  [patch_proceed(): h_now = lax.ppermute(h_now, mesh_name, aux)]
    all_gather x1 -> x0, waiting for transfers between devices: 27.6 us -> none  [body(): gathered = lax.all_gather(attended, 'cand', axis=0, tiled=True)]
    all_gather x1, waiting for transfers between devices: 22.1 us -> 45.1 us  [body(): lax.all_gather(response_value_array, 'seq', axis=1, tiled=True)]
    dot_general x4, matrix products: 23.1 us -> 9.53 us  [attend_block(): jnp.einsum('chgrn,nhd->chgrd', weights, values_split, preferred_element_t...]
    dot_general x4, matrix products: 16.9 us -> 5.01 us  [attend_block(): jnp.einsum('crhgd,nhd->chgrn', query_rows, keys_split, preferred_element_...]
    reduce_sum x7, other arithmetic: 22.3 us -> 13.5 us  [attend_block(): new_total = running_total * rescale + jnp.sum(exponent, axis=-1)]
    ppermute x0 -> x3, local copies, waits for them, and re-layouts: none -> 6.47 us  [patch_proceed(): h_now = lax.ppermute(h_now, mesh_name, aux)]
    all_gather x1, waiting for transfers between devices: 0.01 us -> 5.95 us  [body(): lax.all_gather(response_key_array, 'seq', axis=1, tiled=True)]
  transfers between devices with their start and end apart: 5 -> 7, of which waited for: 4 -> 7; matrix products, arithmetic and copies ran while one was open for 25% -> 15% of each run, Pallas kernels for 0% -> 0%
where the time goes in v1:
time: 313 us; the launch traced here: 312 us
  waiting for transfers between devices  197 us (63%)
  local copies, waits for them, and re-layouts  49.8 us (16%)
  matrix products  27 us (9%)
  other arithmetic  20.2 us (6%)
  between operations  17.1 us (5%)
    all_gather x1, waiting for transfers between devices, body(): lax.all_gather(prompt_value_array, ('cand', 'seq'), axis=0, tiled=True)  58.4 us
    all_gather x1, waiting for transfers between devices, body(): lax.all_gather(prompt_key_array, ('cand', 'seq'), axis=0, tiled=True)  53.8 us
    all_gather x1, waiting for transfers between devices, body(): lax.all_gather(response_value_array, 'seq', axis=1, tiled=True)  45.1 us
    ppermute x3, waiting for transfers between devices, patch_proceed(): h_now = lax.ppermute(h_now, mesh_name, aux)  32.4 us
    unnamed x27, local copies, waits for them, and re-layouts  15.9 us
    reduce_sum x7, other arithmetic, attend_block(): new_total = running_total * rescale + jnp.sum(exponent, axis=-1)  13.5 us
    dynamic_slice x14, local copies, waits for them, and re-layouts, one_block(): lax.dynamic_slice_in_dim(all_values, block_start, block_len, keys_axis)  13.3 us
    dot_general x4, matrix products, attend_block(): jnp.einsum('chgrn,nhd->chgrd', weights, values_split, preferred_element_t...  9.53 us
  transfers between devices with their start and end apart: 7, of which 7 were waited for; matrix products, arithmetic and copies ran while one was open for 15% of the time, Pallas kernels for 0%

profile of v1, /device:TPU:0, one launch (start us, length us, event | category | flops | bytes accessed | tf_op | source)
XLA Modules:
  0.0 312.1 jit_solution(17494399664443600206)
XLA Ops:
  6.5 0.7 all-gather.5.cloned.1.call-update
  7.3 0.7 all-gather.7.cloned.1.call-update
  8.1 1.8 copy.38
  9.9 1.8 copy.39
  11.8 1.7 copy.34
  13.5 1.4 copy.44
  14.9 0.7 copy.36
  15.8 53.8 %all-gather.5.cloned.1.call-done = bf16[2048,512]{1,0:T(8,128)(2,1)} async-done(((bf16[64,512]{1,0:T(8,128)(2,1)}), bf16[2048,512]{1,0:T(8,128)(2,1)}) %all-gather.5.cloned.1.call-update) | async-done | bytes 2097168 | tf_op jit(solution)/shard_map/all_gather | solution.py:106
  69.6 58.4 %all-gather.7.cloned.1.call-done = bf16[2048,512]{1,0:T(8,128)(2,1)} async-done(((bf16[64,512]{1,0:T(8,128)(2,1)}), bf16[2048,512]{1,0:T(8,128)(2,1)}) %all-gather.7.cloned.1.call-update) | async-done | bytes 2097168 | tf_op jit(solution)/shard_map/all_gather | solution.py:107
  128.0 36.4 %while.37 = (s32[]{:T(128)}, f32[2,4,5,96]{3,2,0,1:T(8,128)S(1)}, f32[2,4,5,96]{3,2,0,1:T(8,128)S(1)}, f32[2,4,5,96,128]{4,3,2,0,1:T(8,128)}, s32[2048]{0:T(1024...) while((s32[]{:T(128)}, f32[2,4,5,96]{3,2,0,1:T(8,128)S(1)}, ...), condition=%wide.region_3.4_spmd.clone, body=%wide.region_0.3_spmd.clone.sunk | while | flops 1029754624 | bytes 49735940 | solution.py:81
  128.1 1.3 constant_dynamic-slice_fusion.9
  129.8 1.2 fusion.61
  131.1 2.2 fusion.62
  133.4 2.4 bitcast_add_fusion.2
  135.8 1.3 copy-done.5
  137.2 1.3 constant_dynamic-slice_fusion.9
  139.0 1.2 fusion.61
  140.2 2.2 fusion.62
  142.5 2.4 bitcast_add_fusion.2
  144.9 1.3 copy-done.5
  146.3 1.3 constant_dynamic-slice_fusion.9
  148.0 1.3 fusion.61
  149.3 2.2 fusion.62
  151.6 2.4 bitcast_add_fusion.2
  154.0 1.3 copy-done.5
  155.4 1.3 constant_dynamic-slice_fusion.9
  157.1 1.2 fusion.61
  158.4 2.2 fusion.62
  160.7 2.4 bitcast_add_fusion.2
  163.1 1.3 copy-done.5
  164.4 1.7 copy.42
  166.7 0.6 copy.41
  167.3 5.9 %all-gather.9.cloned.1.call-done = bf16[2,768,512]{2,0,1:T(2,128)(2,1)} async-done(((bf16[2,96,512]{2,0,1:T(2,128)(2,1)}), bf16[2,768,512]{2,0,1:T(2,128)(2,1)}) %all-gather.9.cloned.1.call-update) | async-done | bytes 1572880 | tf_op jit(solution)/shard_map/all_gather | solution.py:135
  173.3 45.1 %all-gather.11.cloned.1.call-done = bf16[2,768,512]{2,0,1:T(2,128)(2,1)} async-done(((bf16[2,96,512]{2,0,1:T(2,128)(2,1)}), bf16[2,768,512]{2,0,1:T(2,128)(2,1)}) %all-gather.11.cloned.1.call-update) | async-done | bytes 1572880 | tf_op jit(solution)/shard_map/all_gather | solution.py:136
  218.3 31.1 %while.36 = (s32[]{:T(128)}, f32[2,4,5,96]{3,2,1,0:T(8,128)}, f32[2,4,5,96]{3,2,1,0:T(8,128)}, f32[2,4,5,96,128]{4,3,2,1,0:T(8,128)S(1)}, s32[768]{0:T(1024)S(1)...) while((s32[]{:T(128)}, f32[2,4,5,96]{3,2,1,0:T(8,128)}, ...), condition=%wide.region_7.8_spmd.clone, body=%wide.region_4.7_spmd.clone.sunk | while | flops 515194976 | bytes 22833208 | solution.py:81
  218.6 0.6 broadcast_and_fusion.2
  219.2 1.9 constant_dynamic-slice_fusion.8
  222.3 2.2 fusion.55
  224.5 1.5 fusion.56
  226.1 2.0 multiply_add_fusion.5
  228.9 0.6 broadcast_and_fusion.2
  229.6 1.9 constant_dynamic-slice_fusion.8
  232.6 2.2 fusion.55
  234.9 1.5 fusion.56
  236.5 2.0 multiply_add_fusion.5
  239.3 0.6 broadcast_and_fusion.2
  240.0 1.9 constant_dynamic-slice_fusion.8
  243.0 2.2 fusion.55
  245.3 1.5 fusion.56
  246.9 2.0 multiply_add_fusion.5
  249.4 2.3 divide_bitcast_fusion
  251.7 1.7 copy.46
  254.7 13.5 %collective-permute-done = bf16[2,96,2560]{2,1,0:T(8,128)(2,1)S(1)} collective-permute-done((bf16[2,96,2560]{2,1,0:T(8,128)(2,1)S(1)}, bf16[2,96,2560]{2,1,0:T(8,128)(2,1)S(1)}, u32[]{:S(2)}, u32[]{:S(2)}) %collective-permute-start) | collective-permute-done | bytes 983072 | tf_op jit(solution)/shard_map/ppermute | solution.py:20
  268.2 0.9 copy-done.8
  269.1 13.6 %collective-permute-done.1 = bf16[2,96,2560]{2,1,0:T(8,128)(2,1)} collective-permute-done((bf16[2,96,2560]{2,1,0:T(8,128)(2,1)S(1)}, bf16[2,96,2560]{2,1,0:T(8,128)(2,1)}, u32[]{:S(2)}, u32[]{:S(2)}) %collective-permute-start.1) | collective-permute-done | bytes 983072 | tf_op jit(solution)/shard_map/ppermute | solution.py:20
  282.7 0.7 fusion.30
  287.2 1.7 copy.50
  288.9 2.4 copy.49
  291.3 5.2 %collective-permute-done.2 = bf16[2,96,2560]{2,1,0:T(8,128)(2,1)} collective-permute-done((bf16[2,96,2560]{2,1,0:T(8,128)(2,1)}, bf16[2,96,2560]{2,1,0:T(8,128)(2,1)}, u32[]{:S(2)}, u32[]{:S(2)}) %collective-permute-start.2) | collective-permute-done | bytes 983072 | tf_op jit(solution)/shard_map/ppermute | solution.py:20
  296.6 2.4 copy.48
  299.0 1.4 constant_dynamic-update-slice_fusion.7
  300.4 1.6 constant_dynamic-update-slice_fusion.6
  302.5 0.8 copy-done.1
  304.2 1.4 copy.54
  (130 shorter events, 12.0 us)
Async XLA Ops:
  6.5 63.1 %all-gather.5.cloned.1.call-start = ((), (), s32[]{:S(2)}) async-start(), calls=%async_computation | async-start | bytes 2162688 | tf_op jit(solution)/shard_map/all_gather | solution.py:106
  7.3 120.7 %all-gather.7.cloned.1.call-start = ((), (), s32[]{:S(2)}) async-start(), calls=%async_computation.1 | async-start | bytes 2162688 | tf_op jit(solution)/shard_map/all_gather | solution.py:107
  8.0 165.2 %all-gather.9.cloned.1.call-start = ((), (), s32[]{:S(2)}) async-start(), calls=%async_computation.2 | async-start | bytes 1769472 | tf_op jit(solution)/shard_map/all_gather | solution.py:135
  9.8 5.7 %copy-start.10 = (s32[8]{0:T(128)S(1)}, s32[8]{0:T(128)}, u32[]{:S(2)}) copy-start(s32[8]{0:T(128)} %param.17) | copy-start | bytes 100
  9.8 5.8 %copy-start.11 = (s32[8]{0:T(128)S(1)}, s32[8]{0:T(128)}, u32[]{:S(2)}) copy-start(s32[8]{0:T(128)} %param.18) | copy-start | bytes 100
  9.9 208.4 %all-gather.11.cloned.1.call-start = ((), (), s32[]{:S(2)}) async-start(), calls=%async_computation.3 | async-start | bytes 1769472 | tf_op jit(solution)/shard_map/all_gather | solution.py:136
  131.1 2.3 copy-start.4
  135.8 1.3 copy-start.5
  140.2 2.3 copy-start.4
  144.9 1.3 copy-start.5
  149.3 2.3 copy-start.4
  154.0 1.3 copy-start.5
  158.4 2.3 copy-start.4
  163.1 1.3 copy-start.5
  222.2 2.2 copy-start.3
  222.2 2.3 copy-start
  222.3 3.8 %copy-start.6 = (f32[2,4,5,96]{3,2,1,0:T(8,128)S(1)}, f32[2,4,5,96]{3,2,1,0:T(8,128)}, u32[]{:S(2)}) copy-start(f32[2,4,5,96]{3,2,1,0:T(8,128)} %get-tuple-element.686) | copy-start | bytes 46084 | tf_op jit(solution)/shard_map/while
  226.1 2.0 copy-start.7
  232.6 2.2 copy-start.3
  232.6 2.3 copy-start
  232.6 3.8 %copy-start.6 = (f32[2,4,5,96]{3,2,1,0:T(8,128)S(1)}, f32[2,4,5,96]{3,2,1,0:T(8,128)}, u32[]{:S(2)}) copy-start(f32[2,4,5,96]{3,2,1,0:T(8,128)} %get-tuple-element.686) | copy-start | bytes 46084 | tf_op jit(solution)/shard_map/while
  236.5 2.0 copy-start.7
  243.0 2.2 copy-start.3
  243.0 2.3 copy-start
  243.0 3.8 %copy-start.6 = (f32[2,4,5,96]{3,2,1,0:T(8,128)S(1)}, f32[2,4,5,96]{3,2,1,0:T(8,128)}, u32[]{:S(2)}) copy-start(f32[2,4,5,96]{3,2,1,0:T(8,128)} %get-tuple-element.686) | copy-start | bytes 46084 | tf_op jit(solution)/shard_map/while
  246.8 2.0 copy-start.7
  251.7 31.0 %copy-start.9 = (s32[8]{0:T(128)S(1)}, s32[8]{0:T(128)}, u32[]{:S(2)}) copy-start(s32[8]{0:T(128)} %param.19) | copy-start | bytes 100
  254.4 13.8 %collective-permute-start = (bf16[2,96,2560]{2,1,0:T(8,128)(2,1)S(1)}, bf16[2,96,2560]{2,1,0:T(8,128)(2,1)S(1)}, u32[]{:S(2)}, u32[]{:S(2)}) collective-permute-start(bf16[2,96,2560]{2,1,0:T(8,128)(2,1)S(1)} %copy.47), channel_id=1, source_target_pairs={{0,8},{8,16},{16,24},{24,0},{1,9},{9,17},{17,25},{25,1},{2,10},{10... | collective-permute-start | bytes 2949128 | tf_op jit(solution)/shard_map/ppermute | solution.py:20
  268.2 0.9 copy-start.8
  269.1 13.6 %collective-permute-start.1 = (bf16[2,96,2560]{2,1,0:T(8,128)(2,1)S(1)}, bf16[2,96,2560]{2,1,0:T(8,128)(2,1)}, u32[]{:S(2)}, u32[]{:S(2)}) collective-permute-start(bf16[2,96,2560]{2,1,0:T(8,128)(2,1)S(1)} %collective-permute-done), channel_id=1, source_target_pairs={{0,8},{8,16},{16,24},{24,0},{1,9},{9,17},{17,25},{25,1},{2,10},{10... | collective-permute-start | bytes 2949128 | tf_op jit(solution)/shard_map/ppermute | solution.py:20
  282.7 13.8 %collective-permute-start.2 = (bf16[2,96,2560]{2,1,0:T(8,128)(2,1)}, bf16[2,96,2560]{2,1,0:T(8,128)(2,1)}, u32[]{:S(2)}, u32[]{:S(2)}) collective-permute-start(bf16[2,96,2560]{2,1,0:T(8,128)(2,1)} %collective-permute-done.1), channel_id=1, source_target_pairs={{0,8},{8,16},{16,24},{24,0},{1,9},{9,17},{17,25},{25,1},{2,10},{10... | collective-permute-start | bytes 2949128 | tf_op jit(solution)/shard_map/ppermute | solution.py:20
  300.4 2.0 copy-start.2
  302.0 1.3 copy-start.1
Sparse Core Ops, SparseCore 0:
  10.3 59.2 all-gather.4
  72.6 55.3 all-gather.6
  130.2 43.0 all-gather.8
  175.3 42.9 all-gather.10
